TPU v7x, 128 devices: a whole 4x4x4 slice. The times are simulated.
128 devices in a mesh: req: 16 (over z, y), mp: 8 (over x, core).
Axes of the slice: x: 4, y: 4, z: 4, core: 2. Of those that a mesh axis runs over, the one named last changes fastest.
Arguments:
- q_pre: bfloat16 [8192, 3072], P('req', 'mp'), may hold values from -64 to 64
- k_pre: bfloat16 [8192, 1024], P('req', 'mp'), may hold values from -64 to 64
- v_pre: bfloat16 [8192, 1024], P('req', 'mp'), may hold values from -12 to 12
- q_bias: float32 [3072], P('mp'), may hold values from -3 to 3
- k_bias: float32 [1024], P('mp'), may hold values from -3 to 3
- v_bias: float32 [1024], P('mp'), may hold values from -3 to 3
- segment_ids: int32 [8192], P('req'), may hold values from -1 to 63, as said below
- lengths: int32 [16, 4], replicated, may hold values from 64 to 128, as said below
- page_table: int32 [16, 4], replicated, may hold values from 0 to 63, as said below
- w_out: bfloat16 [3072, 5120], P('mp'), may hold values from -0.109375 to 0.109375
- residual: bfloat16 [8192, 5120], P('req'), may hold values from -4 to 4
- norm_gain: float32 [5120], replicated, may hold values from 0.1 to 1.9
- w_gate: bfloat16 [5120, 6912], P('req', 'mp'), may hold values from -0.078125 to 0.078125
- w_up: bfloat16 [5120, 6912], P('req', 'mp'), may hold values from -0.078125 to 0.078125
Outputs:
- hidden: bfloat16 [8192, 6912], P('req', 'mp')
- kv_cache: bfloat16 [64, 8, 128, 256], P('req', 'mp')
Inputs may be any that keep to these rules, and one draw needn't show every extreme that they name: Requests of block r lie in order from the block's first token, request j taking lengths[r, j] tokens; in every block one request has exactly 128 tokens. `segment_ids`: token t of block r carries r * 4 + j inside request j's run of tokens given by lengths, and -1 after the last request of its block. `page_table`: every page is named once; page p is held by req index p // 4; the requests of one block have pages held by different req indices.
All inputs are finite; a program needn't handle non-finite values.
Results may differ from a plain program's by a relative error of at most 0.019.
Values may be sent and summed in bfloat16 or wider, within the bound.
A program may use at most 128 MiB of HBM per device.

v0:
```python
import math
import jax
import jax.numpy as jnp
from jax import lax
from jax.sharding import PartitionSpec as P

HD = 128
PAGE = 128
REQS = 4
THETA = 1000000.0
EPS = 1e-06


def rotate(values, positions):
    half_dim = values.shape[-1] // 2
    frequencies = THETA ** (-jnp.arange(half_dim, dtype=jnp.float32) * (2.0 / values.shape[-1]))
    angles = positions[:, None] * frequencies[None, :]
    cosine = jnp.cos(angles)[:, None, :]
    sine_part = jnp.sin(angles)[:, None, :]
    first_half = values[..., :half_dim]
    second = values[..., half_dim:]
    return jnp.concatenate(
        [first_half * cosine - second * sine_part, second * cosine + first_half * sine_part],
        axis=-1,
    )


def attend(queries, keys, values, length):
    scale_factor = 1.0 / math.sqrt(queries.shape[-1])
    scores = (
        jnp.einsum("sqhge,skhe->shgqk", queries, keys, preferred_element_type=jnp.float32)
        * scale_factor
    )
    page_len = queries.shape[1]
    query_pos = jnp.arange(page_len)[:, None]
    key_pos = jnp.arange(page_len)[None, :]
    allowed = (key_pos <= query_pos)[None] & (key_pos[None] < length[:, None, None])
    allowed = allowed[:, None, None]
    row_max = jnp.max(jnp.where(allowed, scores, -1e30), axis=-1, keepdims=True)
    weights = jnp.where(allowed, jnp.exp(scores - row_max), 0.0)
    row_sum = jnp.sum(weights, axis=-1, keepdims=True)
    present = (jnp.arange(page_len)[None, :] < length[:, None])[:, None, None, :, None]
    row_probs = jnp.where(present, weights / jnp.where(present, row_sum, 1.0), 0.0).astype(
        jnp.bfloat16
    )
    mixed_rows = jnp.einsum(
        "shgqk,skhe->sqhge", row_probs, values, preferred_element_type=jnp.float32
    )
    return mixed_rows.astype(jnp.bfloat16)


def normalize(resid_rows, summed, gain_row):
    state = resid_rows.astype(jnp.float32) + summed
    scale_row = lax.rsqrt(jnp.mean(state * state, axis=-1, keepdims=True) + EPS)
    return (state * scale_row * gain_row).astype(jnp.bfloat16)


def shards(
    q_pre,
    k_pre,
    v_pre,
    q_bias,
    k_bias,
    v_bias,
    segment_ids,
    lengths,
    page_table,
    w_out,
    residual,
    norm_gain,
    w_gate,
    w_up,
):
    me_req = lax.axis_index("req")
    groups_all = lax.axis_size("req")
    block_rows = q_pre.shape[0]
    kv_heads = k_pre.shape[1] // HD
    q_heads = q_pre.shape[1] // HD
    group_size = q_heads // kv_heads
    own_lens = lax.dynamic_index_in_dim(lengths, me_req, 0, keepdims=False)
    own_pages = lax.dynamic_index_in_dim(page_table, me_req, 0, keepdims=False)
    own_owner = own_pages // REQS
    starts = jnp.cumsum(own_lens) - own_lens
    offsets = jnp.arange(PAGE, dtype=jnp.int32)
    row_index = jnp.clip(starts[:, None] + offsets[None, :], 0, block_rows - 1)
    flat_index = row_index.reshape(-1)
    request_ids = me_req * REQS + jnp.arange(REQS, dtype=jnp.int32)[:, None]
    inside = (offsets[None, :] < own_lens[:, None]) & (
        jnp.take(segment_ids, flat_index).reshape(REQS, PAGE) == request_ids
    )
    keep_mask = inside[:, :, None, None]
    positions = offsets.astype(jnp.float32)

    def prepare(source, bias_row, head_count):
        picked = jnp.take(source, flat_index, axis=0).astype(jnp.float32) + bias_row
        return picked.reshape(REQS, PAGE, head_count, HD)

    query_req = jnp.where(
        keep_mask, rotate(prepare(q_pre, q_bias, q_heads), positions), 0.0
    ).astype(jnp.bfloat16)
    key_req = jnp.where(keep_mask, rotate(prepare(k_pre, k_bias, kv_heads), positions), 0.0).astype(
        jnp.bfloat16
    )
    value_req = jnp.where(keep_mask, prepare(v_pre, v_bias, kv_heads), 0.0).astype(jnp.bfloat16)
    to_owner = (own_owner[None, :] == jnp.arange(groups_all)[:, None]).astype(jnp.bfloat16)
    alive_rows = segment_ids >= 0
    req_idx = jnp.clip(segment_ids - me_req * REQS, 0, REQS - 1)
    req_hit = req_idx[:, None] == jnp.arange(REQS)[None, :]
    row_start = jnp.sum(jnp.where(req_hit, starts[None, :], 0), axis=1)
    row_pos = jnp.clip(jnp.arange(block_rows, dtype=jnp.int32) - row_start, 0, PAGE - 1)
    hits = (
        page_table[None, :, :] == (me_req * REQS + jnp.arange(REQS, dtype=jnp.int32))[:, None, None]
    )
    page_select = jnp.sum(hits.astype(jnp.int32), axis=2).astype(jnp.bfloat16)
    q_send = jnp.einsum(
        "gj,jpc->gpc",
        to_owner,
        query_req.reshape(REQS, PAGE, q_heads * HD),
        preferred_element_type=jnp.float32,
    ).astype(jnp.bfloat16)
    k_send = jnp.einsum(
        "gj,jpc->gpc",
        to_owner,
        key_req.reshape(REQS, PAGE, kv_heads * HD),
        preferred_element_type=jnp.float32,
    ).astype(jnp.bfloat16)
    v_send = jnp.einsum(
        "gj,jpc->gpc",
        to_owner,
        value_req.reshape(REQS, PAGE, kv_heads * HD),
        preferred_element_type=jnp.float32,
    ).astype(jnp.bfloat16)
    q_in, k_in, v_in = (
        lax.all_to_all(q_send, "req", split_axis=0, concat_axis=0, tiled=True),
        lax.all_to_all(k_send, "req", split_axis=0, concat_axis=0, tiled=True),
        lax.all_to_all(v_send, "req", split_axis=0, concat_axis=0, tiled=True),
    )
    in_len = jnp.sum(jnp.where(page_table // REQS == me_req, lengths, 0), axis=1)
    q_groups = q_in.reshape(groups_all, PAGE, kv_heads, group_size, HD)
    k_groups = k_in.reshape(groups_all, PAGE, kv_heads, HD)
    v_groups = v_in.reshape(groups_all, PAGE, kv_heads, HD)
    pages_in = jnp.concatenate([k_groups, v_groups], axis=-1).transpose(0, 2, 1, 3)
    attended = attend(q_groups, k_groups, v_groups, in_len)
    returned = lax.all_to_all(
        attended.reshape(groups_all, PAGE, q_heads * HD),
        "req",
        split_axis=0,
        concat_axis=0,
        tiled=True,
    )
    row_group = jnp.sum(jnp.where(req_hit, own_owner[None, :], 0), axis=1)
    source_rows = jnp.take(
        returned.reshape(groups_all * PAGE, q_heads * HD), row_group * PAGE + row_pos, axis=0
    )
    cache_out = jnp.einsum(
        "ls,shpc->lhpc", page_select, pages_in, preferred_element_type=jnp.float32
    ).astype(jnp.bfloat16)
    attn_rows = jnp.where(alive_rows[:, None], source_rows, jnp.zeros((), jnp.bfloat16))
    summed = lax.psum(
        jnp.dot(attn_rows, w_out, preferred_element_type=jnp.float32).astype(jnp.bfloat16), "mp"
    ).astype(jnp.float32)
    normed = normalize(residual, summed, norm_gain)
    gate_acc = jnp.dot(
        normed,
        lax.all_gather(w_gate, "req", axis=0, tiled=True),
        preferred_element_type=jnp.float32,
    )
    up_acc = jnp.dot(
        normed, lax.all_gather(w_up, "req", axis=0, tiled=True), preferred_element_type=jnp.float32
    )
    hidden = (jax.nn.silu(gate_acc) * up_acc).astype(jnp.bfloat16)
    return (hidden, cache_out)


def solution(mesh):
    in_specs = (
        P("req", "mp"),
        P("req", "mp"),
        P("req", "mp"),
        P("mp"),
        P("mp"),
        P("mp"),
        P("req"),
        P(),
        P(),
        P("mp", None),
        P("req", None),
        P(),
        P("req", "mp"),
        P("req", "mp"),
    )
    out_specs = (P("req", "mp"), P("req", "mp", None, None))
    return jax.shard_map(shards, mesh=mesh, in_specs=in_specs, out_specs=out_specs, check_vma=False)
```

profile of v0, /device:TPU:1, one launch (start us, length us, event | category | flops | bytes accessed | tf_op | source)
XLA Modules:
  0.0 290.8 jit_solution(10564905103255792273)
XLA Ops:
  8.0 0.9 fusion.29
  9.0 0.1 copy.96
  9.1 0.2 reduce-window.4
  9.3 0.1 add_clamp_fusion
  9.4 0.4 copy-done.14
  9.8 3.6 %gather_fusion = s32[512]{0:T(512)S(1)} fusion(s32[512]{0:T(512)} %param.22, s32[1024]{0:T(1024)S(1)} %pad_clamp_fusion.2), kind=kCustom, calls=%fused_computation.2 | custom fusion | bytes 6144 | tf_op jit(solution)/shard_map/jit(_take)/gather | solution.py:89
  13.4 1.9 gather_fusion.1
  15.3 0.2 copy.78
  15.5 0.1 gather.22
  15.6 0.2 multiply_cosine_fusion
  15.8 0.1 fusion.35
  15.9 0.5 convert_add_fusion.1
  16.4 0.2 multiply_subtract_fusion
  16.6 0.3 pad_maximum_fusion
  17.0 0.1 fusion.10
  17.1 0.2 copy.80
  17.3 0.7 convolution_convert_fusion.2
  18.1 1.5 copy.81
  19.6 8.6 %all-to-all-start.2 = ((bf16[16,128,384]{2,1,0:T(8,128)(2,1)}), bf16[16,128,384]{2,1,0:T(8,128)(2,1)S(1)}, u32[]{:S(2)}, u32[]{:S(2)}) async-start(bf16[16,128,384]{2,1,0:T(8,128)(2,1)} %copy.81), calls=%async_computation.2 | async-start | bytes 3145728 | tf_op jit(solution)/shard_map/all_to_all | solution.py:134
  28.2 0.1 compare_select_fusion.2
  28.3 0.1 compare_and_fusion
  28.4 0.1 copy.74
  28.5 0.1 copy.76
  28.6 0.1 copy.70
  28.8 1.3 gather_fusion.4
  30.1 0.1 convert_add_fusion.2
  30.3 0.1 fusion.52
  30.4 0.4 subtract_bitcast_fusion
  30.8 0.6 convolution_convert_fusion.3
  31.4 0.9 copy.77
  32.4 1.3 gather_fusion.3
  33.8 0.1 convert_add_fusion.3
  33.9 0.6 convolution_convert_fusion.4
  34.5 16.6 %all-to-all-done.2 = bf16[16,128,384]{2,1,0:T(8,128)(2,1)S(1)} async-done(((bf16[16,128,384]{2,1,0:T(8,128)(2,1)}), bf16[16,128,384]{2,1,0:T(8,128)(2,1)S(1)}, u32[]{:S(2)}, u32[]{:S(2)}) %all-to-all-start.2) | async-done | bytes 1572896 | tf_op jit(solution)/shard_map/all_to_all | solution.py:134
  51.1 4.6 %all-to-all-start.1 = ((bf16[16,128,128]{2,1,0:T(8,128)(2,1)}), bf16[16,128,128]{2,1,0:T(8,128)(2,1)S(1)}, u32[]{:S(2)}, u32[]{:S(2)}) async-start(bf16[16,128,128]{2,1,0:T(8,128)(2,1)} %copy.77), calls=%async_computation.1 | async-start | bytes 1048576 | tf_op jit(solution)/shard_map/all_to_all | solution.py:135
  55.7 0.9 copy.72
  56.6 0.1 iota_compare_fusion.1
  56.7 0.3 broadcast_and_fusion
  57.1 1.7 copy.82
  58.7 7.1 %all-to-all-done.1 = bf16[16,128,128]{2,1,0:T(8,128)(2,1)S(1)} async-done(((bf16[16,128,128]{2,1,0:T(8,128)(2,1)}), bf16[16,128,128]{2,1,0:T(8,128)(2,1)S(1)}, u32[]{:S(2)}, u32[]{:S(2)}) %all-to-all-start.1) | async-done | bytes 524320 | tf_op jit(solution)/shard_map/all_to_all | solution.py:135
  65.8 4.2 %all-to-all-start = ((bf16[16,128,128]{2,1,0:T(8,128)(2,1)}), bf16[16,128,128]{2,1,0:T(8,128)(2,1)}, u32[]{:S(2)}, u32[]{:S(2)}) async-start(bf16[16,128,128]{2,1,0:T(8,128)(2,1)} %copy.72), calls=%async_computation | async-start | bytes 1048576 | tf_op jit(solution)/shard_map/all_to_all | solution.py:136
  70.1 2.2 fusion
  72.3 0.9 fusion.3
  73.2 6.2 %all-to-all-done = bf16[16,128,128]{2,1,0:T(8,128)(2,1)} async-done(((bf16[16,128,128]{2,1,0:T(8,128)(2,1)}), bf16[16,128,128]{2,1,0:T(8,128)(2,1)}, u32[]{:S(2)}, u32[]{:S(2)}) %all-to-all-start) | async-done | bytes 524320 | tf_op jit(solution)/shard_map/all_to_all | solution.py:136
  79.4 3.3 %convolution_convert_fusion.1 = bf16[16,128,3,128]{3,1,2,0:T(8,128)(2,1)} fusion(f32[16,128,128,3]{2,1,3,0:T(8,128)S(1)} %get-tuple-element.24, f32[16,3,128]{2,1,0:T(4,128)S(1)} %broadcast_select_fusion, f32[16,3,128]{2,1,0:T(4,128)S(1)} %get-tuple-element.23, pred[16,128,128]{1,2,0:T(8,128)(4,1)S(1)} %broadcast_and_fusion, ...), kind=kOutput, calls=%fused_computation.17 | convolution fusion | flops 206831616 | bytes 5556224 | tf_op jit(solution)/shard_map/shgqk,skhe->sqhge/dot_general | solution.py:46
  82.7 4.0 %all-to-all-start.3 = ((bf16[16,128,384]{1,2,0:T(8,128)(2,1)}), bf16[16,128,384]{1,2,0:T(8,128)(2,1)S(1)}, u32[]{:S(2)}, u32[]{:S(2)}) async-start(bf16[16,128,384]{1,2,0:T(8,128)(2,1)} %bitcast.106), calls=%async_computation.3 | async-start | bytes 3145728 | tf_op jit(solution)/shard_map/all_to_all | solution.py:144
  86.8 0.1 select_reduce_fusion
  87.0 0.5 compare_and_fusion.2
  87.5 18.7 %all-to-all-done.3 = bf16[16,128,384]{1,2,0:T(8,128)(2,1)S(1)} async-done(((bf16[16,128,384]{1,2,0:T(8,128)(2,1)}), bf16[16,128,384]{1,2,0:T(8,128)(2,1)S(1)}, u32[]{:S(2)}, u32[]{:S(2)}) %all-to-all-start.3) | async-done | bytes 1572896 | tf_op jit(solution)/shard_map/all_to_all | solution.py:144
  106.2 0.9 copy.86
  107.1 1.9 gather_fusion.2
  109.1 6.9 %convolution_convert_fusion = bf16[512,5120]{1,0:T(8,128)(2,1)} fusion(bf16[384,5120]{1,0:T(8,128)(2,1)} %param.25, bf16[512,384]{1,0:T(8,128)(2,1)S(1)} %gather_fusion.2, pred[512]{0:T(512)(128)(4,1)S(1)} %copy-done.12, pred[512]{0:T(512)(128)(4,1)S(1)} %broadcast_compare_fusion), kind=kOutput, calls=%fused_computation.8 | convolution fusion | flops 2016280576 | bytes 9569280 | tf_op jit(solution)/shard_map/dot_general | solution.py:160
  116.1 0.5 all-gather.3.cloned.1.call-update
  116.6 0.5 all-gather.5.cloned.1.call-update
  117.2 0.1 convert_reduce_fusion
  117.3 0.3 copy.110
  117.6 1.4 copy.109
  119.0 0.3 fusion.7
  119.3 0.7 copy.89
  120.0 74.5 %all-reduce.2.cloned.1.call-done = bf16[512,5120]{1,0:T(8,128)(2,1)} async-done(((bf16[512,5120]{1,0:T(8,128)(2,1)}), bf16[512,5120]{1,0:T(8,128)(2,1)}) %all-reduce.2.cloned.1.call-update) | async-done | bytes 5242896 | tf_op jit(solution)/shard_map/psum | solution.py:159
  194.5 5.8 %multiply_reduce_fusion = f32[512]{0:T(512)S(1)} fusion(bf16[512,5120]{1,0:T(8,128)(2,1)} %all-reduce.2.cloned.1.call-done, bf16[512,5120]{1,0:T(8,128)(2,1)} %param.26), kind=kLoop, calls=%fused_computation.6 | loop fusion | flops 13106688 | bytes 10487808 | tf_op jit(solution)/shard_map/reduce_sum | solution.py:54
  200.4 12.1 %fusion.51 = f32[512,864]{0,1:T(8,128)S(1)} fusion(bf16[5120,864]{1,0:T(8,128)(2,1)} %all-gather.3.cloned.1.call-done, bf16[512,5120]{1,0:T(8,128)(2,1)} %all-reduce.2.cloned.1.call-done, bf16[512,5120]{1,0:T(8,128)(2,1)} %param.26, f32[5120]{0:T(1024)S(1)} %copy-done.13, f32[512]{0:T(512)S(1)} %add_rsqrt_fusion), kind=kOutput, calls=%fused_computation.124 | convolution fusion | flops 4545576960 | bytes 21125120 | tf_op jit(solution)/shard_map/dot_general | solution.py:163
  212.5 58.1 %all-gather.5.cloned.1.call-done = bf16[5120,864]{1,0:T(8,128)(2,1)} async-done(((bf16[320,864]{1,0:T(8,128)(2,1)}), bf16[5120,864]{1,0:T(8,128)(2,1)}) %all-gather.5.cloned.1.call-update) | async-done | bytes 8847376 | tf_op jit(solution)/shard_map/all_gather | solution.py:169
  270.6 12.8 %multiply_convert_fusion.1 = bf16[512,864]{0,1:T(8,128)(2,1)} fusion(f32[512,864]{0,1:T(8,128)S(1)} %fusion.51, bf16[5120,864]{1,0:T(8,128)(2,1)} %all-gather.5.cloned.1.call-done, bf16[512,5120]{1,0:T(8,128)(2,1)} %all-reduce.2.cloned.1.call-done, bf16[512,5120]{1,0:T(8,128)(2,1)} %param.26, f32[5120]{0:T(1024)S(1)} %copy-done.13, f32[512]{0:T(512)S(1)} %add_rsqrt_fusion), kind=kOutput, calls=%fused_computation.16 | convolution fusion | flops 4548231168 | bytes 22009856 | tf_op jit(solution)/shard_map/dot_general | solution.py:168
  (54 shorter events, 0.5 us)
Async XLA Ops:
  8.0 5.4 %copy-start = (bf16[512,384]{1,0:T(8,128)(2,1)S(1)}, bf16[512,384]{1,0:T(8,128)(2,1)}, u32[]{:S(2)}) copy-start(bf16[512,384]{1,0:T(8,128)(2,1)} %param.16) | copy-start | bytes 1179652
  9.3 0.5 copy-start.14
  9.8 6.2 %copy-start.9 = (f32[384]{0:T(512)S(1)}, f32[384]{0:T(512)}, u32[]{:S(2)}) copy-start(f32[384]{0:T(512)} %param.19) | copy-start | bytes 4612
  18.1 10.7 %copy-start.3 = (bf16[512,128]{1,0:T(8,128)(2,1)S(1)}, bf16[512,128]{1,0:T(8,128)(2,1)}, u32[]{:S(2)}) copy-start(bf16[512,128]{1,0:T(8,128)(2,1)} %param.17) | copy-start | bytes 393220
  18.1 12.0 %copy-start.10 = (f32[128]{0:T(128)S(1)}, f32[128]{0:T(128)}, u32[]{:S(2)}) copy-start(f32[128]{0:T(128)} %param.20) | copy-start | bytes 1540
  19.6 31.5 %all-to-all-start.2 = ((bf16[16,128,384]{2,1,0:T(8,128)(2,1)}), bf16[16,128,384]{2,1,0:T(8,128)(2,1)S(1)}, u32[]{:S(2)}, u32[]{:S(2)}) async-start(bf16[16,128,384]{2,1,0:T(8,128)(2,1)} %copy.81), calls=%async_computation.2 | async-start | bytes 3145728 | tf_op jit(solution)/shard_map/all_to_all | solution.py:134
  28.2 4.2 %copy-start.4 = (bf16[512,128]{1,0:T(8,128)(2,1)S(1)}, bf16[512,128]{1,0:T(8,128)(2,1)}, u32[]{:S(2)}) copy-start(bf16[512,128]{1,0:T(8,128)(2,1)} %param.18) | copy-start | bytes 393220
  28.7 5.0 %copy-start.7 = (s32[16,4]{0,1:T(4,128)S(1)}, s32[16,4]{0,1:T(4,128)}, u32[]{:S(2)}) copy-start(s32[16,4]{0,1:T(4,128)} %param.24) | copy-start | bytes 772
  28.8 5.0 %copy-start.8 = (s32[16,4]{0,1:T(4,128)S(1)}, s32[16,4]{0,1:T(4,128)}, u32[]{:S(2)}) copy-start(s32[16,4]{0,1:T(4,128)} %param.23) | copy-start | bytes 772
  28.8 5.0 %copy-start.11 = (f32[128]{0:T(128)S(1)}, f32[128]{0:T(128)}, u32[]{:S(2)}) copy-start(f32[128]{0:T(128)} %param.21) | copy-start | bytes 1540
  51.1 14.7 %all-to-all-start.1 = ((bf16[16,128,128]{2,1,0:T(8,128)(2,1)}), bf16[16,128,128]{2,1,0:T(8,128)(2,1)S(1)}, u32[]{:S(2)}, u32[]{:S(2)}) async-start(bf16[16,128,128]{2,1,0:T(8,128)(2,1)} %copy.77), calls=%async_computation.1 | async-start | bytes 1048576 | tf_op jit(solution)/shard_map/all_to_all | solution.py:135
  65.8 4.2 %copy-start.5 = (bf16[16,128,128]{2,1,0:T(8,128)(2,1)}, bf16[16,128,128]{2,1,0:T(8,128)(2,1)S(1)}, u32[]{:S(2)}) copy-start(bf16[16,128,128]{2,1,0:T(8,128)(2,1)S(1)} %all-to-all-done.1) | copy-start | bytes 1572868
  65.8 13.6 %all-to-all-start = ((bf16[16,128,128]{2,1,0:T(8,128)(2,1)}), bf16[16,128,128]{2,1,0:T(8,128)(2,1)}, u32[]{:S(2)}, u32[]{:S(2)}) async-start(bf16[16,128,128]{2,1,0:T(8,128)(2,1)} %copy.72), calls=%async_computation | async-start | bytes 1048576 | tf_op jit(solution)/shard_map/all_to_all | solution.py:136
  82.7 4.1 %copy-start.15 = (s32[4,1]{0,1:T(1,128)S(1)}, s32[4,1]{0,1:T(1,128)}, u32[]{:S(2)}) copy-start(s32[4,1]{0,1:T(1,128)} %copy-done.14) | copy-start | bytes 52
  82.7 4.1 %copy-start.2 = (s32[512]{0:T(512)S(1)}, s32[512]{0:T(512)}, u32[]{:S(2)}) copy-start(s32[512]{0:T(512)} %param.22) | copy-start | bytes 6148
  82.7 23.5 %all-to-all-start.3 = ((bf16[16,128,384]{1,2,0:T(8,128)(2,1)}), bf16[16,128,384]{1,2,0:T(8,128)(2,1)S(1)}, u32[]{:S(2)}, u32[]{:S(2)}) async-start(bf16[16,128,384]{1,2,0:T(8,128)(2,1)} %bitcast.106), calls=%async_computation.3 | async-start | bytes 3145728 | tf_op jit(solution)/shard_map/all_to_all | solution.py:144
  86.7 107.8 %all-reduce.2.cloned.1.call-start = ((), (), s32[]{:S(2)}) async-start(), calls=%async_computation.4 | async-start | bytes 10485760 | tf_op jit(solution)/shard_map/psum | solution.py:159
  107.1 2.0 copy-start.12
  116.0 1.3 copy-start.6
  116.0 84.4 %all-gather.3.cloned.1.call-start = ((), (), s32[]{:S(2)}) async-start(), calls=%async_computation.5 | async-start | bytes 9748480 | tf_op jit(solution)/shard_map/all_gather | solution.py:165
  116.6 154.0 %all-gather.5.cloned.1.call-start = ((), (), s32[]{:S(2)}) async-start(), calls=%async_computation.6 | async-start | bytes 9748480 | tf_op jit(solution)/shard_map/all_gather | solution.py:169
  120.0 80.4 %copy-start.13 = (f32[5120]{0:T(1024)S(1)}, f32[5120]{0:T(1024)}, u32[]{:S(2)}) copy-start(f32[5120]{0:T(1024)} %param.27) | copy-start | bytes 61444
  270.6 12.8 %copy-start.1 = (bf16[512,384]{1,0:T(8,128)(2,1)S(1)}, bf16[512,384]{1,0:T(8,128)(2,1)}, u32[]{:S(2)}) copy-start(bf16[512,384]{1,0:T(8,128)(2,1)} %param.16) | copy-start | bytes 1179652
Sparse Core Ops, SparseCore 0:
  116.1 78.3 all-reduce.1
Sparse Core Ops, SparseCore 1:
  118.6 75.8 all-gather.2
  196.5 74.0 all-gather.4
where the time goes:
time: 291 us
  waiting for transfers between devices  182 us (63%)
  matrix products  39.5 us (14%)
  starting transfers between devices  21.5 us (7%)
  local copies, waits for them, and re-layouts  20.2 us (7%)
  between operations  16 us (5%)
  other arithmetic  11.3 us (4%)
    psum x1, waiting for transfers between devices, shards(): lax.psum(jnp.dot(attn_rows, w_out, preferred_element_type=jnp.float32).as...  74.5 us
    all_gather x1, waiting for transfers between devices, shards(): lax.all_gather(w_up, 'req', axis=0, tiled=True)  58.1 us
    all_to_all x1, waiting for transfers between devices, shards(): lax.all_to_all(attended.reshape(groups_all, PAGE, q_heads * HD), 'req', s...  18.7 us
    all_to_all x1, waiting for transfers between devices, shards(): lax.all_to_all(q_send, 'req', split_axis=0, concat_axis=0, tiled=True)  16.6 us
    dot_general x1, matrix products, shards(): jnp.dot(normed, lax.all_gather(w_up, 'req', axis=0, tiled=True), preferre...  12.8 us
    dot_general x1, matrix products, shards(): jnp.dot(normed, lax.all_gather(w_gate, 'req', axis=0, tiled=True), prefer...  12.1 us
    all_to_all x1, starting transfers between devices, shards(): lax.all_to_all(q_send, 'req', split_axis=0, concat_axis=0, tiled=True)  8.6 us
    all_to_all x1, waiting for transfers between devices, shards(): lax.all_to_all(k_send, 'req', split_axis=0, concat_axis=0, tiled=True)  7.09 us
  transfers between devices with their start and end apart: 7, of which 6 were waited for; matrix products, arithmetic and copies ran while one was open for 12% of the time, Pallas kernels for 0%

commit v1 on v0

--- a/solution.py
+++ b/solution.py
@@ -1,3 +1,4 @@
+import functools
 import math
 import jax
 import jax.numpy as jnp
@@ -9,6 +10,14 @@
 REQS = 4
 THETA = 1000000.0
 EPS = 1e-06
+
+
+def draft_unit(in_array, axis_key):
+    step_out = jnp.sum(lax.all_gather(in_array, axis_key), axis=0)
+    return step_out
+
+
+push_tracks = functools.partial(draft_unit, axis_key="mp")
 
 
 def rotate(values, positions):
@@ -156,8 +165,8 @@
         "ls,shpc->lhpc", page_select, pages_in, preferred_element_type=jnp.float32
     ).astype(jnp.bfloat16)
     attn_rows = jnp.where(alive_rows[:, None], source_rows, jnp.zeros((), jnp.bfloat16))
-    summed = lax.psum(
-        jnp.dot(attn_rows, w_out, preferred_element_type=jnp.float32).astype(jnp.bfloat16), "mp"
+    summed = push_tracks(
+        jnp.dot(attn_rows, w_out, preferred_element_type=jnp.float32).astype(jnp.bfloat16)
     ).astype(jnp.float32)
     normed = normalize(residual, summed, norm_gain)
     gate_acc = jnp.dot(

time: 291 us -> 482 us (1.66)
  waiting for transfers between devices: 182 us -> 356 us
  other arithmetic: 11.3 us -> 29.4 us
    all_gather x0 -> x1, waiting for transfers between devices: none -> 190 us  [draft_unit(): step_out = jnp.sum(lax.all_gather(in_array, axis_key), axis=0)]
    psum x1 -> x0, waiting for transfers between devices: 74.5 us -> none  [shards(): lax.psum(jnp.dot(attn_rows, w_out, preferred_element_type=jnp.float32).as...]
    all_gather x1, waiting for transfers between devices: 0.02 us -> 51.7 us  [shards(): lax.all_gather(w_gate, 'req', axis=0, tiled=True)]
    reduce_sum x0 -> x1, other arithmetic: none -> 17.9 us  [draft_unit(): step_out = jnp.sum(lax.all_gather(in_array, axis_key), axis=0)]
    all_gather x1, waiting for transfers between devices: 58.1 us -> 64.2 us  [shards(): lax.all_gather(w_up, 'req', axis=0, tiled=True)]
  transfers between devices with their start and end apart: 7 -> 7, of which waited for: 6 -> 7; matrix products, arithmetic and copies ran while one was open for 12% -> 11% of each run, Pallas kernels for 0% -> 0%
where the time goes in v1:
time: 482 us; the launch traced here: 481 us
  waiting for transfers between devices  356 us (74%)
  matrix products  39.6 us (8%)
  other arithmetic  29.4 us (6%)
  starting transfers between devices  21.5 us (4%)
  local copies, waits for them, and re-layouts  20.2 us (4%)
  between operations  14.2 us (3%)
    all_gather x1, waiting for transfers between devices, draft_unit(): step_out = jnp.sum(lax.all_gather(in_array, axis_key), axis=0)  190 us
    all_gather x1, waiting for transfers between devices, shards(): lax.all_gather(w_up, 'req', axis=0, tiled=True)  64.2 us
    all_gather x1, waiting for transfers between devices, shards(): lax.all_gather(w_gate, 'req', axis=0, tiled=True)  51.7 us
    all_to_all x1, waiting for transfers between devices, shards(): lax.all_to_all(attended.reshape(groups_all, PAGE, q_heads * HD), 'req', s...  18.7 us
    reduce_sum x1, other arithmetic, draft_unit(): step_out = jnp.sum(lax.all_gather(in_array, axis_key), axis=0)  17.9 us
    all_to_all x1, waiting for transfers between devices, shards(): lax.all_to_all(q_send, 'req', split_axis=0, concat_axis=0, tiled=True)  16.6 us
    dot_general x1, matrix products, shards(): jnp.dot(normed, lax.all_gather(w_up, 'req', axis=0, tiled=True), preferre...  12.8 us
    dot_general x1, matrix products, shards(): jnp.dot(normed, lax.all_gather(w_gate, 'req', axis=0, tiled=True), prefer...  12.1 us
  transfers between devices with their start and end apart: 7, of which 7 were waited for; matrix products, arithmetic and copies ran while one was open for 11% of the time, Pallas kernels for 0%

profile of v1, /device:TPU:1, one launch (start us, length us, event | category | flops | bytes accessed | tf_op | source)
XLA Modules:
  0.0 480.9 jit_solution(12087201406264020254)
XLA Ops:
  7.2 0.9 fusion.29
  8.1 0.1 copy.96
  8.2 0.2 reduce-window.4
  8.4 0.1 add_clamp_fusion
  8.5 0.4 copy-done.14
  8.9 3.6 gather_fusion
  12.6 1.9 gather_fusion.1
  14.5 0.2 copy.78
  14.7 0.1 gather.22
  14.8 0.2 multiply_cosine_fusion
  15.0 0.1 fusion.35
  15.1 0.5 convert_add_fusion.1
  15.6 0.2 multiply_subtract_fusion
  15.8 0.3 pad_maximum_fusion
  16.1 0.1 fusion.10
  16.3 0.2 copy.80
  16.5 0.7 convolution_convert_fusion.2
  17.3 1.5 copy.81
  18.8 8.6 %all-to-all-start.2 = ((bf16[16,128,384]{2,1,0:T(8,128)(2,1)}), bf16[16,128,384]{2,1,0:T(8,128)(2,1)S(1)}, u32[]{:S(2)}, u32[]{:S(2)}) async-start(bf16[16,128,384]{2,1,0:T(8,128)(2,1)} %copy.81), calls=%async_computation.2 | async-start | bytes 3145728 | tf_op jit(solution)/shard_map/all_to_all | solution.py:143
  27.5 0.1 compare_and_fusion
  27.6 0.1 copy.74
  27.7 0.1 copy.76
  27.8 0.1 copy.70
  28.0 1.3 gather_fusion.4
  29.3 0.1 convert_add_fusion.2
  29.5 0.1 fusion.52
  29.6 0.4 subtract_bitcast_fusion
  30.0 0.6 convolution_convert_fusion.3
  30.6 0.9 copy.77
  31.5 1.3 gather_fusion.3
  32.9 0.1 convert_add_fusion.3
  33.1 0.6 convolution_convert_fusion.4
  33.7 16.6 %all-to-all-done.2 = bf16[16,128,384]{2,1,0:T(8,128)(2,1)S(1)} async-done(((bf16[16,128,384]{2,1,0:T(8,128)(2,1)}), bf16[16,128,384]{2,1,0:T(8,128)(2,1)S(1)}, u32[]{:S(2)}, u32[]{:S(2)}) %all-to-all-start.2) | async-done | bytes 1572896 | tf_op jit(solution)/shard_map/all_to_all | solution.py:143
  50.3 4.6 all-to-all-start.1
  54.9 0.9 copy.72
  55.9 0.3 broadcast_and_fusion
  56.2 1.7 copy.82
  57.9 7.1 %all-to-all-done.1 = bf16[16,128,128]{2,1,0:T(8,128)(2,1)S(1)} async-done(((bf16[16,128,128]{2,1,0:T(8,128)(2,1)}), bf16[16,128,128]{2,1,0:T(8,128)(2,1)S(1)}, u32[]{:S(2)}, u32[]{:S(2)}) %all-to-all-start.1) | async-done | bytes 524320 | tf_op jit(solution)/shard_map/all_to_all | solution.py:144
  65.0 4.2 all-to-all-start
  69.2 2.2 fusion
  71.5 0.9 fusion.3
  72.4 6.2 %all-to-all-done = bf16[16,128,128]{2,1,0:T(8,128)(2,1)} async-done(((bf16[16,128,128]{2,1,0:T(8,128)(2,1)}), bf16[16,128,128]{2,1,0:T(8,128)(2,1)}, u32[]{:S(2)}, u32[]{:S(2)}) %all-to-all-start) | async-done | bytes 524320 | tf_op jit(solution)/shard_map/all_to_all | solution.py:145
  78.5 3.3 convolution_convert_fusion.1
  81.9 4.0 all-to-all-start.3
  86.0 0.1 select_reduce_fusion
  86.2 0.5 compare_and_fusion.2
  86.7 18.7 %all-to-all-done.3 = bf16[16,128,384]{1,2,0:T(8,128)(2,1)S(1)} async-done(((bf16[16,128,384]{1,2,0:T(8,128)(2,1)}), bf16[16,128,384]{1,2,0:T(8,128)(2,1)S(1)}, u32[]{:S(2)}, u32[]{:S(2)}) %all-to-all-start.3) | async-done | bytes 1572896 | tf_op jit(solution)/shard_map/all_to_all | solution.py:153
  105.4 0.9 copy.86
  106.3 1.9 gather_fusion.2
  108.2 7.0 %convolution_convert_fusion = bf16[512,5120]{1,0:T(8,128)(2,1)} fusion(bf16[384,5120]{1,0:T(8,128)(2,1)} %param.25, bf16[512,384]{1,0:T(8,128)(2,1)S(1)} %gather_fusion.2, pred[512]{0:T(512)(128)(4,1)S(1)} %copy-done.12, pred[512]{0:T(512)(128)(4,1)S(1)} %broadcast_compare_fusion), kind=kOutput, calls=%fused_computation.8 | convolution fusion | flops 2016280576 | bytes 9569280 | tf_op jit(solution)/shard_map/dot_general | solution.py:169
  115.3 0.7 all-gather.5.cloned.1.call-update
  116.0 0.7 all-gather.7.cloned.1.call-update
  116.7 0.1 convert_reduce_fusion
  116.8 0.3 copy.110
  117.2 1.4 copy.109
  118.5 0.3 fusion.7
  118.8 0.7 copy.89
  119.6 190.2 %all-gather.9.cloned.1.call-done = bf16[4096,5120]{1,0:T(8,128)(2,1)} async-done(((bf16[512,5120]{1,0:T(8,128)(2,1)}), bf16[4096,5120]{1,0:T(8,128)(2,1)}) %all-gather.9.cloned.1.call-update) | async-done | bytes 41943056 | tf_op jit(solution)/shard_map/all_gather | solution.py:16
  309.7 17.9 %reduce_sum.73 = bf16[512,5120]{1,0:T(8,128)(2,1)} reduce(bf16[8,512,5120]{2,1,0:T(8,128)(2,1)} %bitcast.104, bf16[]{:T(256)} %constant.123.clone.1), dimensions={0}, to_apply=%region_6.8 | reduce | flops 18350080 | bytes 47185920 | tf_op jit(solution)/shard_map/reduce_sum | solution.py:16
  327.7 6.0 %multiply_reduce_fusion = f32[512]{0:T(512)S(1)} fusion(bf16[512,5120]{1,0:T(8,128)(2,1)} %reduce_sum.73, bf16[512,5120]{1,0:T(8,128)(2,1)} %param.26), kind=kLoop, calls=%fused_computation.6 | loop fusion | flops 13106688 | bytes 10487808 | tf_op jit(solution)/shard_map/reduce_sum | solution.py:63
  333.7 51.7 %all-gather.5.cloned.1.call-done = bf16[5120,864]{1,0:T(8,128)(2,1)} async-done(((bf16[320,864]{1,0:T(8,128)(2,1)}), bf16[5120,864]{1,0:T(8,128)(2,1)}) %all-gather.5.cloned.1.call-update) | async-done | bytes 8847376 | tf_op jit(solution)/shard_map/all_gather | solution.py:174
  385.4 12.1 %fusion.51 = f32[512,864]{0,1:T(8,128)S(1)} fusion(bf16[5120,864]{1,0:T(8,128)(2,1)} %all-gather.5.cloned.1.call-done, bf16[512,5120]{1,0:T(8,128)(2,1)} %reduce_sum.73, bf16[512,5120]{1,0:T(8,128)(2,1)} %param.26, f32[5120]{0:T(1024)S(1)} %copy-done.13, f32[512]{0:T(512)S(1)} %add_rsqrt_fusion), kind=kOutput, calls=%fused_computation.124 | convolution fusion | flops 4545576960 | bytes 21125120 | tf_op jit(solution)/shard_map/dot_general | solution.py:172
  397.4 64.2 %all-gather.7.cloned.1.call-done = bf16[5120,864]{1,0:T(8,128)(2,1)} async-done(((bf16[320,864]{1,0:T(8,128)(2,1)}), bf16[5120,864]{1,0:T(8,128)(2,1)}) %all-gather.7.cloned.1.call-update) | async-done | bytes 8847376 | tf_op jit(solution)/shard_map/all_gather | solution.py:178
  461.6 12.8 %multiply_convert_fusion.1 = bf16[512,864]{0,1:T(8,128)(2,1)} fusion(f32[512,864]{0,1:T(8,128)S(1)} %fusion.51, bf16[5120,864]{1,0:T(8,128)(2,1)} %all-gather.7.cloned.1.call-done, bf16[512,5120]{1,0:T(8,128)(2,1)} %reduce_sum.73, bf16[512,5120]{1,0:T(8,128)(2,1)} %param.26, f32[5120]{0:T(1024)S(1)} %copy-done.13, f32[512]{0:T(512)S(1)} %add_rsqrt_fusion), kind=kOutput, calls=%fused_computation.16 | convolution fusion | flops 4548231168 | bytes 22009856 | tf_op jit(solution)/shard_map/dot_general | solution.py:177
  (55 shorter events, 0.6 us)
Async XLA Ops:
  7.2 5.4 %copy-start = (bf16[512,384]{1,0:T(8,128)(2,1)S(1)}, bf16[512,384]{1,0:T(8,128)(2,1)}, u32[]{:S(2)}) copy-start(bf16[512,384]{1,0:T(8,128)(2,1)} %param.16) | copy-start | bytes 1179652
  8.4 0.5 copy-start.14
  8.9 6.2 %copy-start.9 = (f32[384]{0:T(512)S(1)}, f32[384]{0:T(512)}, u32[]{:S(2)}) copy-start(f32[384]{0:T(512)} %param.19) | copy-start | bytes 4612
  17.2 10.7 %copy-start.3 = (bf16[512,128]{1,0:T(8,128)(2,1)S(1)}, bf16[512,128]{1,0:T(8,128)(2,1)}, u32[]{:S(2)}) copy-start(bf16[512,128]{1,0:T(8,128)(2,1)} %param.17) | copy-start | bytes 393220
  17.3 12.0 %copy-start.10 = (f32[128]{0:T(128)S(1)}, f32[128]{0:T(128)}, u32[]{:S(2)}) copy-start(f32[128]{0:T(128)} %param.20) | copy-start | bytes 1540
  18.8 31.5 %all-to-all-start.2 = ((bf16[16,128,384]{2,1,0:T(8,128)(2,1)}), bf16[16,128,384]{2,1,0:T(8,128)(2,1)S(1)}, u32[]{:S(2)}, u32[]{:S(2)}) async-start(bf16[16,128,384]{2,1,0:T(8,128)(2,1)} %copy.81), calls=%async_computation.2 | async-start | bytes 3145728 | tf_op jit(solution)/shard_map/all_to_all | solution.py:143
  27.4 4.2 copy-start.4
  27.9 5.0 %copy-start.7 = (s32[16,4]{0,1:T(4,128)S(1)}, s32[16,4]{0,1:T(4,128)}, u32[]{:S(2)}) copy-start(s32[16,4]{0,1:T(4,128)} %param.24) | copy-start | bytes 772
  27.9 5.0 %copy-start.8 = (s32[16,4]{0,1:T(4,128)S(1)}, s32[16,4]{0,1:T(4,128)}, u32[]{:S(2)}) copy-start(s32[16,4]{0,1:T(4,128)} %param.23) | copy-start | bytes 772
  27.9 5.0 %copy-start.11 = (f32[128]{0:T(128)S(1)}, f32[128]{0:T(128)}, u32[]{:S(2)}) copy-start(f32[128]{0:T(128)} %param.21) | copy-start | bytes 1540
  50.3 14.7 %all-to-all-start.1 = ((bf16[16,128,128]{2,1,0:T(8,128)(2,1)}), bf16[16,128,128]{2,1,0:T(8,128)(2,1)S(1)}, u32[]{:S(2)}, u32[]{:S(2)}) async-start(bf16[16,128,128]{2,1,0:T(8,128)(2,1)} %copy.77), calls=%async_computation.1 | async-start | bytes 1048576 | tf_op jit(solution)/shard_map/all_to_all | solution.py:144
  65.0 4.2 copy-start.5
  65.0 13.6 %all-to-all-start = ((bf16[16,128,128]{2,1,0:T(8,128)(2,1)}), bf16[16,128,128]{2,1,0:T(8,128)(2,1)}, u32[]{:S(2)}, u32[]{:S(2)}) async-start(bf16[16,128,128]{2,1,0:T(8,128)(2,1)} %copy.72), calls=%async_computation | async-start | bytes 1048576 | tf_op jit(solution)/shard_map/all_to_all | solution.py:145
  81.9 4.1 copy-start.15
  81.9 4.1 copy-start.2
  81.9 23.5 %all-to-all-start.3 = ((bf16[16,128,384]{1,2,0:T(8,128)(2,1)}), bf16[16,128,384]{1,2,0:T(8,128)(2,1)S(1)}, u32[]{:S(2)}, u32[]{:S(2)}) async-start(bf16[16,128,384]{1,2,0:T(8,128)(2,1)} %bitcast.108), calls=%async_computation.3 | async-start | bytes 3145728 | tf_op jit(solution)/shard_map/all_to_all | solution.py:153
  85.9 223.8 %all-gather.9.cloned.1.call-start = ((), (), s32[]{:S(2)}) async-start(), calls=%async_computation.6 | async-start | bytes 47185920 | tf_op jit(solution)/shard_map/all_gather | solution.py:16
  106.3 2.0 copy-start.12
  115.2 1.6 copy-start.6
  115.2 270.1 %all-gather.5.cloned.1.call-start = ((), (), s32[]{:S(2)}) async-start(), calls=%async_computation.4 | async-start | bytes 9748480 | tf_op jit(solution)/shard_map/all_gather | solution.py:174
  116.0 345.6 %all-gather.7.cloned.1.call-start = ((), (), s32[]{:S(2)}) async-start(), calls=%async_computation.5 | async-start | bytes 9748480 | tf_op jit(solution)/shard_map/all_gather | solution.py:178
  327.7 57.7 %copy-start.13 = (f32[5120]{0:T(1024)S(1)}, f32[5120]{0:T(1024)}, u32[]{:S(2)}) copy-start(f32[5120]{0:T(1024)} %param.27) | copy-start | bytes 61444
  461.6 12.8 %copy-start.1 = (bf16[512,384]{1,0:T(8,128)(2,1)S(1)}, bf16[512,384]{1,0:T(8,128)(2,1)}, u32[]{:S(2)}) copy-start(bf16[512,384]{1,0:T(8,128)(2,1)} %param.16) | copy-start | bytes 1179652
Sparse Core Ops, SparseCore 0:
  115.3 194.3 all-gather.8
  311.9 73.4 all-gather.4
  387.5 74.0 all-gather.6
